TPU v7x, 32 devices: a whole 2x2x4 slice. The times are simulated.
32 devices in a mesh: row: 4 (over y, x), col: 8 (over z, core).
Axes of the slice: x: 2, y: 2, z: 4, core: 2. Of those that a mesh axis runs over, the one named last changes fastest.
Arguments:
- known_inverse: float32 [12288, 12288], P('col', 'row'), may hold values from -6 to 6
- factor_sep: float32 [12288, 1536], P('col'), may hold values from -0.09375 to 0.09375
- factor_pair: float32 [1536, 1536], P('col'), may hold values from -0.25 to 0.25
- pivot_inverse: float32 [1536, 1536], P('col', 'row'), may hold values from -6 to 6
- widths: int32 [8], replicated, may hold values from 1 to 512, 1536 in all
- parent_of: int32 [8], replicated, may hold values from -1 to 7, as said below
- ancestors: int32 [8, 24], replicated, may hold values from 0 to 63, all different within a row
Outputs:
- panel_inverse: float32 [1536, 12288], P('col', 'row')
- block_inverse: float32 [1536, 1536], P('col', 'row')
Inputs may be any that keep to these rules, and one draw needn't show every extreme that they name: `parent_of`: exactly 4 supernodes have -1; each other one names one of those. `ancestors`: each supernode lists different blocks; every block is listed by some supernode. The widths sum to 1536.
All inputs are finite; a program needn't handle non-finite values.
Results may differ from a plain program's by a relative error of at most 0.0003.
Values sent between devices are 32-bit elements; how exact they have to be, the bound alone decides.
A program may use at most 192 MiB of HBM per device.

v0:
```python
import jax
import jax.numpy as jnp
from jax import lax
from jax.sharding import PartitionSpec as P

NS = 12288
WTOT = 1536
NSUP = 8
NBLK = 64


exact_mode = lax.Precision.HIGHEST


def spread(x, axis, root):
    mine = lax.axis_index(axis) == root
    return lax.psum(jnp.where(mine, x, jnp.zeros_like(x)), axis)


def plain_dot(left, right):
    return jnp.dot(left, right, precision=exact_mode, preferred_element_type=jnp.float32)


def first_dot(left, right):
    return lax.dot_general(
        left,
        right,
        (((0,), (0,)), ((), ())),
        precision=exact_mode,
        preferred_element_type=jnp.float32,
    )


def supernode_tables(widths, parent_of, ancestors):
    position = jnp.arange(WTOT, dtype=jnp.int32)
    width_ends = jnp.cumsum(widths)
    column_owner = jnp.sum((width_ends[None, :] <= position[:, None]).astype(jnp.int32), axis=1)
    owner_onehot = column_owner[:, None] == jnp.arange(NSUP, dtype=jnp.int32)[None, :]
    listed = jnp.any(
        ancestors[:, :, None] == jnp.arange(NBLK, dtype=jnp.int32)[None, None, :], axis=1
    ).astype(jnp.float32)
    column_blocks = plain_dot(owner_onehot.astype(jnp.float32), listed)
    column_parent = jnp.sum(jnp.where(owner_onehot, parent_of[None, :], 0), axis=1)
    column_upper = column_parent < 0
    return (column_owner, column_blocks, column_parent, column_upper)


def shards(known_inverse, factor_sep, factor_pair, pivot_inverse, widths, parent_of, ancestors):
    col_index = lax.axis_index("col")
    row_index = lax.axis_index("row")
    fold_ratio = lax.axis_size("col") // lax.axis_size("row")
    sep_local = factor_sep.shape[0]
    pair_local = factor_pair.shape[0]
    wide_local = pivot_inverse.shape[1]
    column_owner, column_blocks, column_parent, column_upper = supernode_tables(
        widths, parent_of, ancestors
    )
    sep_index = col_index * sep_local + jnp.arange(sep_local, dtype=jnp.int32)
    block_onehot = (
        (sep_index // (NS // NBLK))[:, None] == jnp.arange(NBLK, dtype=jnp.int32)[None, :]
    ).astype(jnp.float32)
    sep_factor = factor_sep * plain_dot(block_onehot, column_blocks.T)
    upper_cols = column_upper.astype(jnp.float32)
    lower_cols = 1.0 - upper_cols
    owner_rows = lax.dynamic_slice_in_dim(column_owner, col_index * pair_local, pair_local)
    owner_wide = lax.dynamic_slice_in_dim(column_owner, row_index * wide_local, wide_local)
    parent_wide = lax.dynamic_slice_in_dim(column_parent, row_index * wide_local, wide_local)
    upper_rows = lax.dynamic_slice_in_dim(upper_cols, col_index * pair_local, pair_local)
    upper_wide = lax.dynamic_slice_in_dim(column_upper, row_index * wide_local, wide_local)
    coupling = jnp.where(
        (owner_rows[:, None] == column_parent[None, :]) & (~column_upper)[None, :], factor_pair, 0.0
    )
    matching = owner_rows[:, None] == owner_wide[None, :]
    match_upper = matching & upper_wide[None, :]
    match_lower = matching & (~upper_wide)[None, :]
    match_pair = owner_rows[:, None] == parent_wide[None, :]
    sep_pieces = []
    pair_pieces = []
    for turn in range(fold_ratio):
        got_sep, got_pair = (
            spread(sep_factor, "col", row_index * fold_ratio + turn),
            spread(coupling, "col", row_index * fold_ratio + turn),
        )
        sep_pieces.append(got_sep)
        pair_pieces.append(got_pair)
    sep_cols = jnp.concatenate(sep_pieces, 0)
    coupling_cols = jnp.concatenate(pair_pieces, 0)
    coupling_own = lax.dynamic_slice_in_dim(coupling, row_index * wide_local, wide_local, 1)

    def supernode_sums(term):
        return lax.psum_scatter(
            term(jnp.int32(0), pair_local * lax.axis_size("col")),
            "col",
            scatter_dimension=0,
            tiled=True,
        )

    def panel_term(lead):

        def term(start, count):
            return first_dot(lead, known_inverse)

        return term

    coupling_all = lax.all_gather(coupling, "col", axis=0, tiled=True)
    lead = sep_factor - plain_dot(sep_factor * upper_cols[None, :], coupling_all)
    panel = -supernode_sums(panel_term(lead))
    panel_upper = panel * upper_rows[:, None]
    pivot_part = pivot_inverse - lax.psum_scatter(
        plain_dot(panel, sep_cols), "row", scatter_dimension=1, tiled=True
    )
    upper_block = jnp.where(match_upper, pivot_part, 0.0)
    pair_rows = -lax.psum(
        plain_dot(panel_upper, sep_cols * lower_cols[None, :])
        + plain_dot(upper_block, coupling_cols),
        "row",
    )
    pair_block = jnp.where(
        match_pair, lax.dynamic_slice_in_dim(pair_rows, row_index * wide_local, wide_local, 1), 0.0
    )

    def pair_term(start, count):
        return first_dot(pair_rows, coupling_own)

    lower_block = jnp.where(match_lower, pivot_part - supernode_sums(pair_term), 0.0)
    return (panel, upper_block + lower_block + pair_block)


def solution(mesh):
    in_specs = (P("col", "row"), P("col", None), P("col", None), P("col", "row"), P(), P(), P())
    out_specs = (P("col", "row"), P("col", "row"))
    return jax.shard_map(shards, mesh=mesh, in_specs=in_specs, out_specs=out_specs, check_vma=False)
```

profile of v0, /device:TPU:0, one launch (start us, length us, event | category | flops | bytes accessed | tf_op | source)
XLA Modules:
  0.0 875.7 jit_solution(11107905401404456032)
XLA Ops:
  7.2 0.0 all-gather.2.cloned.1.call-start
  7.2 0.8 reduce-window.8
  8.0 0.1 convert_reduce_fusion
  8.1 0.7 select_reduce_fusion
  8.9 0.6 broadcast_subtract_fusion
  9.5 0.0 copy-start.8
  9.5 0.0 copy-start.7
  9.5 0.5 copy-done.8
  10.0 0.1 dynamic_slice.21
  10.1 0.0 copy-start.5
  10.1 0.5 copy-done.5
  10.6 0.0 copy-start.10
  10.6 3.0 broadcast_select_fusion.3
  13.6 0.0 copy-start.1
  13.6 0.0 all-gather.2.cloned.1.call-update
  13.6 0.0 all-reduce.6.cloned.1.call-start
  13.7 0.0 copy-done.10
  13.7 0.1 fusion.22
  13.8 0.4 fusion.23
  14.3 0.6 copy-done.1
  14.9 1.1 broadcast_select_fusion.2
  16.0 15.3 %broadcast_select_fusion = (f32[1536,1536]{1,0:T(8,128)}, f32[1536,1536]{1,0:T(8,128)}, f32[1536,1536]{1,0:T(8,128)}) fusion(pred[]{:T(512)S(6)} %eq.100, pred[]{:T(512)S(6)} %eq.99, f32[1536,1536]{1,0:T(8,128)} %param.8, f32[1536,64]{1,0:T(8,128)S(1)} %fusion.23, s32[1536]{0:T(1024)S(1)} %add_select_fusion), kind=kOutput, calls=%fused_computation.8 | convolution fusion | flops 1819115520 | bytes 38148096 | tf_op jit(solution)/shard_map/dot_general | solution.py:21
  31.3 0.0 all-reduce.6.cloned.1.call-update
  31.3 0.0 reduce-scatter.4.cloned.1.call-start
  31.3 75.9 %all-gather.2.cloned.1.call-done = f32[1536,1536]{1,0:T(8,128)} async-done(((f32[192,1536]{1,0:T(8,128)}), f32[1536,1536]{1,0:T(8,128)}) %all-gather.2.cloned.1.call-update) | async-done | bytes 9437200 | tf_op jit(solution)/shard_map/all_gather | solution.py:105
  107.2 0.0 copy-done.7
  107.2 51.9 %fusion.5 = f32[1536,1536]{1,0:T(8,128)} fusion(f32[1536,1536]{1,0:T(8,128)} %all-gather.2.cloned.1.call-done, f32[1536,1536]{1,0:T(8,128)} %get-tuple-element.16, f32[1536]{0:T(1024)S(1)} %get-tuple-element.14), kind=kOutput, calls=%fused_computation.6 | convolution fusion | flops 43488903168 | bytes 28317696 | tf_op jit(solution)/shard_map/dot_general | solution.py:21
  159.2 98.5 %fusion.3 = f32[1536,3072]{1,0:T(8,128)} fusion(f32[1536,3072]{1,0:T(8,128)} %param.7, f32[1536,1536]{1,0:T(8,128)} %get-tuple-element.16, f32[1536,1536]{1,0:T(8,128)} %fusion.5), kind=kOutput, calls=%fused_computation.4 | convolution fusion | flops 86975447040 | bytes 56623104 | tf_op jit(solution)/shard_map/dot_general | solution.py:25
  257.7 0.0 reduce-scatter.4.cloned.1.call-update
  257.7 0.0 reduce-scatter.6.cloned.1.call-start
  257.7 268.0 %all-reduce.6.cloned.1.call-done = (f32[1536,1536]{1,0:T(8,128)}, f32[1536,1536]{1,0:T(8,128)}, f32[192,1536]{1,0:T(8,128)}, f32[192,1536]{1,0:T(8,128)}) async-done(((f32[1536,1536]{1,0:T(8,128)}, f32[1536,1536]{1,0:T(8,128)}, f32[192,1536]{1,0:T(8,128)}, f32[192,1536]{1,0:T(8,128)}), (f32[1536,1536]{1,0:T(8,128)}, f32[1536,1536]{1,0:T(8,128)}, f32[192,1536]{1,0:T(8,128)}, ...) | async-done | bytes 21233680 | tf_op jit(solution)/shard_map/psum | solution.py:17
  525.8 0.0 copy-start.2
  525.8 9.5 %constant_dynamic-update-slice_fusion.1 = f32[3072,1536]{1,0:T(8,128)} fusion(f32[1536,1536]{1,0:T(8,128)} %get-tuple-element.2), kind=kLoop, calls=%fused_computation.46 | loop fusion | bytes 18874368
  535.2 0.0 copy-done.2
  535.2 4.5 constant_dynamic-update-slice_fusion
  539.7 176.4 %reduce-scatter.4.cloned.1.call-done = f32[192,3072]{1,0:T(8,128)} async-done(((f32[1536,3072]{1,0:T(8,128)}), f32[192,3072]{1,0:T(8,128)}) %reduce-scatter.4.cloned.1.call-update) | async-done | bytes 2359312 | tf_op jit(solution)/shard_map/reduce_scatter | solution.py:91
  716.2 1.8 neg.6
  718.0 0.0 copy-start
  718.0 17.5 %fusion.32 = f32[192,1536]{1,0:T(8,128)} fusion(f32[192,3072]{1,0:T(8,128)S(1)} %neg.6, f32[3072,1536]{1,0:T(8,128)} %constant_dynamic-update-slice_fusion), kind=kOutput, calls=%fused_computation.55 | convolution fusion | flops 10871635968 | bytes 22413312 | tf_op jit(solution)/shard_map/dot_general | solution.py:21
  735.6 0.0 reduce-scatter.6.cloned.1.call-update
  735.6 0.0 all-reduce.4.cloned.1.call-start
  735.7 1.4 dynamic_slice.24
  737.0 0.7 dynamic_slice.22
  737.7 1.2 fusion.30
  738.9 0.0 copy-done
  738.9 0.0 copy-start.4
  738.9 17.7 %fusion = f32[192,1536]{1,0:T(8,128)} fusion(f32[3072,1536]{1,0:T(8,128)} %constant_dynamic-update-slice_fusion, f32[1536]{0:T(1024)} %get-tuple-element.8, f32[192,3072]{1,0:T(8,128)S(1)} %neg.6, f32[192]{0:T(256)} %dynamic_slice.24), kind=kOutput, calls=%fused_computation | convolution fusion | flops 10876944384 | bytes 22420224 | tf_op jit(solution)/shard_map/dot_general | solution.py:21
  756.6 6.4 reduce-scatter.6.cloned.1.call-done
  763.0 1.1 sub.27
  764.1 0.0 copy-done.4
  764.1 0.0 copy-done.6
  764.1 5.2 convolution_add_fusion
  769.3 0.0 all-reduce.4.cloned.1.call-update
  769.3 0.0 reduce-scatter.8.cloned.1.call-start
  769.3 54.5 %all-reduce.4.cloned.1.call-done = f32[192,1536]{1,0:T(8,128)} async-done(((f32[192,1536]{1,0:T(8,128)}), f32[192,1536]{1,0:T(8,128)}) %all-reduce.4.cloned.1.call-update) | async-done | bytes 1179664 | tf_op jit(solution)/shard_map/psum | solution.py:113
  823.9 5.5 fusion.14
  829.4 0.0 reduce-scatter.8.cloned.1.call-update
  829.4 0.1 dynamic_slice.26
  829.5 0.0 copy-done.3
  829.5 0.1 neg.7
  829.6 37.0 %reduce-scatter.8.cloned.1.call-done = f32[192,384]{1,0:T(8,128)} async-done(((f32[1536,384]{1,0:T(8,128)}), f32[192,384]{1,0:T(8,128)}) %reduce-scatter.8.cloned.1.call-update) | async-done | bytes 294928 | tf_op jit(solution)/shard_map/reduce_scatter | solution.py:91
  866.6 0.0 copy-done.9
  866.6 0.0 copy-done.11
  866.6 1.9 select_add_fusion
  (6 shorter events, 0.0 us)
Async XLA Ops:
  7.2 100.1 %all-gather.2.cloned.1.call-start = ((), (), s32[]{:S(2)}) async-start(), calls=%async_computation.3 | async-start | bytes 10616832 | tf_op jit(solution)/shard_map/all_gather | solution.py:105
  9.5 0.5 copy-start.8
  9.5 97.7 %copy-start.7 = (f32[1536]{0:T(1024)}, f32[1536]{0:T(1024)S(1)}, u32[]{:S(2)}) copy-start(f32[1536]{0:T(1024)S(1)} %get-tuple-element.14) | copy-start | bytes 18436
  10.1 0.5 copy-start.5
  10.6 3.1 copy-start.10
  13.6 1.3 copy-start.1
  13.6 512.1 %all-reduce.6.cloned.1.call-start = ((), (), s32[]{:S(2)}) async-start(), calls=%async_computation.8 | async-start | bytes 42467328 | tf_op jit(solution)/shard_map/psum | solution.py:17
  31.3 684.9 %reduce-scatter.4.cloned.1.call-start = ((), (), s32[]{:S(2)}) async-start(), calls=%async_computation.4 | async-start | bytes 21233664 | tf_op jit(solution)/shard_map/reduce_scatter | solution.py:91
  257.7 505.3 %reduce-scatter.6.cloned.1.call-start = ((), (), s32[]{:S(2)}) async-start(), calls=%async_computation.5 | async-start | bytes 1474560 | tf_op jit(solution)/shard_map/reduce_scatter | solution.py:109
  525.8 9.5 %copy-start.2 = (f32[1536,1536]{1,0:T(8,128)S(1)}, f32[1536,1536]{1,0:T(8,128)}, u32[]{:S(2)}) copy-start(f32[1536,1536]{1,0:T(8,128)} %get-tuple-element.3) | copy-start | bytes 28311556
  718.0 20.9 %copy-start = (f32[192,3072]{1,0:T(8,128)}, f32[192,3072]{1,0:T(8,128)S(1)}, u32[]{:S(2)}) copy-start(f32[192,3072]{1,0:T(8,128)S(1)} %neg.6) | copy-start | bytes 7077892
  735.6 88.3 %all-reduce.4.cloned.1.call-start = ((), (), s32[]{:S(2)}) async-start(), calls=%async_computation.6 | async-start | bytes 2359296 | tf_op jit(solution)/shard_map/psum | solution.py:113
  738.9 25.2 %copy-start.4 = (s32[384]{0:T(512)S(1)}, s32[384]{0:T(512)}, u32[]{:S(2)}) copy-start(s32[384]{0:T(512)} %dynamic_slice.22) | copy-start | bytes 4612
  738.9 25.2 %copy-start.6 = (s32[192]{0:T(256)S(1)}, s32[192]{0:T(256)}, u32[]{:S(2)}) copy-start(s32[192]{0:T(256)} %copy-done.5) | copy-start | bytes 2308
  769.3 97.3 %reduce-scatter.8.cloned.1.call-start = ((), (), s32[]{:S(2)}) async-start(), calls=%async_computation.7 | async-start | bytes 2654208 | tf_op jit(solution)/shard_map/reduce_scatter | solution.py:91
  823.9 5.6 copy-start.3
  829.4 37.2 %copy-start.9 = (pred[384]{0:T(512)(128)(4,1)S(1)}, pred[384]{0:T(512)(128)(4,1)}, u32[]{:S(2)}) copy-start(pred[384]{0:T(512)(128)(4,1)} %get-tuple-element.7) | copy-start | bytes 1156
  829.4 37.2 %copy-start.11 = (pred[384]{0:T(512)(128)(4,1)S(1)}, pred[384]{0:T(512)(128)(4,1)}, u32[]{:S(2)}) copy-start(pred[384]{0:T(512)(128)(4,1)} %get-tuple-element.6) | copy-start | bytes 1156
Sparse Core Ops, SparseCore 0:
  13.8 93.4 all-gather.1
  110.7 415.0 all-reduce.5
  528.1 188.0 reduce-scatter.3
  735.7 27.2 reduce-scatter.5
  769.4 54.4 all-reduce.3
  829.5 37.0 reduce-scatter.7
where the time goes:
time: 881 us; the launch traced here: 876 us
  waiting for transfers between devices  618 us (70%)
  matrix products  212 us (24%)
  local copies, waits for them, and re-layouts  17.9 us (2%)
  between operations  14.6 us (2%)
  other arithmetic  12.6 us (1%)
    psum x1, waiting for transfers between devices, spread(): return lax.psum(jnp.where(mine, x, jnp.zeros_like(x)), axis)  268 us
    reduce_scatter x2, waiting for transfers between devices, supernode_sums(): lax.psum_scatter(term(jnp.int32(0), pair_local * lax.axis_size('col')), '...  213 us
    dot_general x6, matrix products, plain_dot(): jnp.dot(left, right, precision=exact_mode, preferred_element_type=jnp.flo...  108 us
    dot_general x2, matrix products, first_dot(): lax.dot_general(left, right, (((0,), (0,)), ((), ())), precision=exact_mo...  104 us
    all_gather x1, waiting for transfers between devices, shards(): coupling_all = lax.all_gather(coupling, 'col', axis=0, tiled=True)  75.9 us
    psum x1, waiting for transfers between devices, shards(): lax.psum(plain_dot(panel_upper, sep_cols * lower_cols[None, :]) + plain_d...  54.5 us
  transfers between devices with their start and end apart: 6, of which 6 were waited for; matrix products, arithmetic and copies ran while one was open for 23% of the time, Pallas kernels for 0%

commit v1 on v0

--- a/solution.py
+++ b/solution.py
@@ -9,12 +9,8 @@
 NBLK = 64
 
 
-exact_mode = lax.Precision.HIGHEST
-
-
-def spread(x, axis, root):
-    mine = lax.axis_index(axis) == root
-    return lax.psum(jnp.where(mine, x, jnp.zeros_like(x)), axis)
+exact_mode = lax.Precision.HIGH
+panel_chunks = 4
 
 
 def plain_dot(left, right):
@@ -48,7 +44,9 @@
 def shards(known_inverse, factor_sep, factor_pair, pivot_inverse, widths, parent_of, ancestors):
     col_index = lax.axis_index("col")
     row_index = lax.axis_index("row")
-    fold_ratio = lax.axis_size("col") // lax.axis_size("row")
+    rows = lax.axis_size("row")
+    cols = lax.axis_size("col")
+    fold_ratio = cols // rows
     sep_local = factor_sep.shape[0]
     pair_local = factor_pair.shape[0]
     wide_local = pivot_inverse.shape[1]
@@ -71,59 +69,54 @@
         (owner_rows[:, None] == column_parent[None, :]) & (~column_upper)[None, :], factor_pair, 0.0
     )
     matching = owner_rows[:, None] == owner_wide[None, :]
-    match_upper = matching & upper_wide[None, :]
     match_lower = matching & (~upper_wide)[None, :]
     match_pair = owner_rows[:, None] == parent_wide[None, :]
-    sep_pieces = []
-    pair_pieces = []
-    for turn in range(fold_ratio):
-        got_sep, got_pair = (
-            spread(sep_factor, "col", row_index * fold_ratio + turn),
-            spread(coupling, "col", row_index * fold_ratio + turn),
-        )
-        sep_pieces.append(got_sep)
-        pair_pieces.append(got_pair)
-    sep_cols = jnp.concatenate(sep_pieces, 0)
-    coupling_cols = jnp.concatenate(pair_pieces, 0)
-    coupling_own = lax.dynamic_slice_in_dim(coupling, row_index * wide_local, wide_local, 1)
-
-    def supernode_sums(term):
-        return lax.psum_scatter(
-            term(jnp.int32(0), pair_local * lax.axis_size("col")),
-            "col",
-            scatter_dimension=0,
-            tiled=True,
-        )
-
-    def panel_term(lead):
-
-        def term(start, count):
-            return first_dot(lead, known_inverse)
-
-        return term
+    match_upper_all = (owner_rows[:, None] == column_owner[None, :]) & column_upper[None, :]
 
     coupling_all = lax.all_gather(coupling, "col", axis=0, tiled=True)
-    lead = sep_factor - plain_dot(sep_factor * upper_cols[None, :], coupling_all)
-    panel = -supernode_sums(panel_term(lead))
-    panel_upper = panel * upper_rows[:, None]
-    pivot_part = pivot_inverse - lax.psum_scatter(
-        plain_dot(panel, sep_cols), "row", scatter_dimension=1, tiled=True
+
+    piece_rows = sep_local // rows
+    piece = lax.dynamic_slice_in_dim(sep_factor, row_index * piece_rows, piece_rows)
+    deal = [
+        (r * cols + c, (c // fold_ratio) * cols + (c % fold_ratio) * rows + r)
+        for r in range(rows)
+        for c in range(cols)
+    ]
+    piece = lax.ppermute(piece, ("row", "col"), deal)
+    piece, coupling_all = lax.optimization_barrier((piece, coupling_all))
+    sep_cols = lax.all_gather(piece, "col", axis=0, tiled=True)
+
+    lead = plain_dot(sep_factor * upper_cols[None, :], coupling_all) - sep_factor
+    step = known_inverse.shape[1] // panel_chunks
+    panels = []
+    product = jnp.zeros((pair_local, WTOT), jnp.float32)
+    for i in range(panel_chunks):
+        part = first_dot(lead, known_inverse[:, i * step : (i + 1) * step])
+        panels.append(lax.psum_scatter(part, "col", scatter_dimension=0, tiled=True))
+    for i in range(panel_chunks):
+        product = product + plain_dot(panels[i], sep_cols[i * step : (i + 1) * step])
+    panel = jnp.concatenate(panels, 1)
+
+    own_pivot = lax.dynamic_update_slice_in_dim(
+        jnp.zeros_like(product), jnp.where(matching, pivot_inverse, 0.0), row_index * wide_local, 1
     )
-    upper_block = jnp.where(match_upper, pivot_part, 0.0)
-    pair_rows = -lax.psum(
-        plain_dot(panel_upper, sep_cols * lower_cols[None, :])
-        + plain_dot(upper_block, coupling_cols),
-        "row",
+    deficit = lax.psum(product - own_pivot, "row")
+    upper_block_all = jnp.where(match_upper_all, -deficit, 0.0)
+    pair_rows = -(
+        deficit * upper_rows[:, None] * lower_cols[None, :]
+        + plain_dot(upper_block_all, coupling_all)
     )
-    pair_block = jnp.where(
-        match_pair, lax.dynamic_slice_in_dim(pair_rows, row_index * wide_local, wide_local, 1), 0.0
+    pair_cols = lax.all_to_all(pair_rows, "col", split_axis=1, concat_axis=0, tiled=True)
+    coupling_own = lax.dynamic_slice_in_dim(coupling_all, row_index * wide_local, wide_local, 1)
+
+    def own_cols(x):
+        return lax.dynamic_slice_in_dim(x, row_index * wide_local, wide_local, 1)
+
+    pair_block = jnp.where(match_pair, own_cols(pair_rows), 0.0)
+    lower_block = jnp.where(
+        match_lower, -own_cols(deficit) - first_dot(pair_cols, coupling_own), 0.0
     )
-
-    def pair_term(start, count):
-        return first_dot(pair_rows, coupling_own)
-
-    lower_block = jnp.where(match_lower, pivot_part - supernode_sums(pair_term), 0.0)
-    return (panel, upper_block + lower_block + pair_block)
+    return (panel, own_cols(upper_block_all) + lower_block + pair_block)
 
 
 def solution(mesh):

time: 881 us -> 759 us (0.86)
  matrix products: 212 us -> 146 us
  waiting for transfers between devices: 618 us -> 561 us
    psum x2 -> x1, waiting for transfers between devices: 323 us -> 52.2 us  [shards(): deficit = lax.psum(product - own_pivot, 'row')]
    all_gather x0 -> x1, waiting for transfers between devices: none -> 169 us  [shards(): sep_cols = lax.all_gather(piece, 'col', axis=0, tiled=True)]
    all_gather x1, waiting for transfers between devices: 75.9 us -> 147 us  [shards(): coupling_all = lax.all_gather(coupling, 'col', axis=0, tiled=True)]
    reduce_scatter x3 -> x4, waiting for transfers between devices: 220 us -> 159 us  [shards(): lax.psum_scatter(part, 'col', scatter_dimension=0, tiled=True)]
    dot_general x6 -> x8, matrix products: 108 us -> 62.3 us  [plain_dot(): jnp.dot(left, right, precision=exact_mode, preferred_element_type=jnp.flo...]
    all_to_all x0 -> x1, waiting for transfers between devices: none -> 33.2 us  [shards(): lax.all_to_all(pair_rows, 'col', split_axis=1, concat_axis=0, tiled=True)]
    dot_general x2 -> x5, matrix products: 104 us -> 83.6 us  [first_dot(): lax.dot_general(left, right, (((0,), (0,)), ((), ())), precision=exact_mo...]
  transfers between devices with their start and end apart: 6 -> 9, of which waited for: 6 -> 8; matrix products, arithmetic and copies ran while one was open for 23% -> 11% of each run, Pallas kernels for 0% -> 0%
where the time goes in v1:
time: 759 us; the launch traced here: 752 us
  waiting for transfers between devices  561 us (74%)
  matrix products  146 us (19%)
  between operations  14.8 us (2%)
  local copies, waits for them, and re-layouts  12.9 us (2%)
  other arithmetic  10.9 us (1%)
    all_gather x1, waiting for transfers between devices, shards(): sep_cols = lax.all_gather(piece, 'col', axis=0, tiled=True)  169 us
    reduce_scatter x4, waiting for transfers between devices, shards(): lax.psum_scatter(part, 'col', scatter_dimension=0, tiled=True)  159 us
    all_gather x1, waiting for transfers between devices, shards(): coupling_all = lax.all_gather(coupling, 'col', axis=0, tiled=True)  147 us
    dot_general x5, matrix products, first_dot(): lax.dot_general(left, right, (((0,), (0,)), ((), ())), precision=exact_mo...  83.6 us
    dot_general x8, matrix products, plain_dot(): jnp.dot(left, right, precision=exact_mode, preferred_element_type=jnp.flo...  62.3 us
    psum x1, waiting for transfers between devices, shards(): deficit = lax.psum(product - own_pivot, 'row')  52.2 us
    all_to_all x1, waiting for transfers between devices, shards(): lax.all_to_all(pair_rows, 'col', split_axis=1, concat_axis=0, tiled=True)  33.2 us
  transfers between devices with their start and end apart: 9, of which 8 were waited for; matrix products, arithmetic and copies ran while one was open for 11% of the time, Pallas kernels for 0%

profile of v1, /device:TPU:0, one launch (start us, length us, event | category | flops | bytes accessed | tf_op | source)
XLA Modules:
  0.0 751.8 jit_solution(14991458933092573735)
XLA Ops:
  7.2 0.0 all-gather.3.cloned.1.call-start
  7.2 0.8 reduce-window.8
  8.0 0.1 convert_reduce_fusion
  8.1 0.7 select_reduce_fusion
  8.9 0.1 dynamic_slice.31
  9.0 0.6 broadcast_subtract_fusion
  9.6 2.6 and_select_fusion
  12.2 0.0 all-gather.3.cloned.1.call-update
  12.2 0.0 reduce-scatter.9.cloned.1.call-start
  12.2 0.0 copy-done.9
  12.3 0.8 fusion.51
  13.1 0.3 fusion.52
  13.3 5.8 convolution_multiply_fusion
  19.1 0.0 copy-start
  19.1 3.8 copy-done
  22.9 0.2 constant_dynamic-slice_fusion
  23.1 0.8 collective-permute-start
  23.9 0.0 collective-permute-done
  23.9 0.0 copy-start.4
  23.9 147.2 %all-gather.3.cloned.1.call-done = f32[1536,1536]{1,0:T(8,128)} async-done(((f32[192,1536]{1,0:T(8,128)}), f32[1536,1536]{1,0:T(8,128)}) %all-gather.3.cloned.1.call-update) | async-done | bytes 9437200 | tf_op jit(solution)/shard_map/all_gather | solution.py:76
  171.1 29.8 %fusion.2 = f32[1536,1536]{1,0:T(8,128)S(1)} fusion(f32[1536,1536]{1,0:T(8,128)} %copy-done, f32[1536,1536]{1,0:T(8,128)} %all-gather.3.cloned.1.call-done, f32[1536]{0:T(1024)S(1)} %get-tuple-element.8), kind=kOutput, calls=%fused_computation.3 | convolution fusion | flops 21747990528 | bytes 28317696 | tf_op jit(solution)/shard_map/dot_general | solution.py:17
  201.0 3.7 copy-done.14
  204.6 26.7 %fusion.15 = f32[1536,768]{1,0:T(8,128)} fusion(f32[1536,1536]{1,0:T(8,128)S(1)} %fusion.2, f32[1536,3072]{1,0:T(8,128)} %param.7), kind=kOutput, calls=%fused_computation.14 | convolution fusion | flops 10871635968 | bytes 18874368 | tf_op jit(solution)/shard_map/dot_general | solution.py:21
  231.3 0.0 reduce-scatter.9.cloned.1.call-update
  231.3 0.0 all-gather.5.cloned.1.call-start
  231.4 0.7 all-gather.5.cloned.1.call-update
  232.1 0.0 reduce-scatter.7.cloned.1.call-start
  232.1 17.8 %fusion.17 = f32[1536,768]{1,0:T(8,128)} fusion(f32[1536,1536]{1,0:T(8,128)} %copy-done.14, f32[1536,3072]{1,0:T(8,128)} %param.7), kind=kOutput, calls=%fused_computation.16 | convolution fusion | flops 10871635968 | bytes 18874368 | tf_op jit(solution)/shard_map/dot_general | solution.py:21
  249.9 0.0 reduce-scatter.7.cloned.1.call-update
  250.0 0.0 reduce-scatter.5.cloned.1.call-start
  250.0 17.6 %fusion.19 = f32[1536,768]{1,0:T(8,128)} fusion(f32[1536,1536]{1,0:T(8,128)} %copy-done.14, f32[1536,3072]{1,0:T(8,128)} %param.7), kind=kOutput, calls=%fused_computation.18 | convolution fusion | flops 10871635968 | bytes 18874368 | tf_op jit(solution)/shard_map/dot_general | solution.py:21
  267.7 0.0 reduce-scatter.5.cloned.1.call-update
  267.7 0.0 reduce-scatter.11.cloned.1.call-start
  267.7 17.7 %fusion.13 = f32[1536,768]{1,0:T(8,128)} fusion(f32[1536,1536]{1,0:T(8,128)} %copy-done.14, f32[1536,3072]{1,0:T(8,128)} %param.7), kind=kOutput, calls=%fused_computation.12 | convolution fusion | flops 10871635968 | bytes 18874368 | tf_op jit(solution)/shard_map/dot_general | solution.py:21
  285.4 0.0 reduce-scatter.11.cloned.1.call-update
  285.4 0.3 all-reduce.2.cloned.1.call-start
  285.7 0.1 dynamic_slice.32
  285.8 1.2 broadcast_in_dim.24
  286.9 0.8 fusion.50
  287.8 5.4 reduce-scatter.9.cloned.1.call-done
  293.1 169.0 %all-gather.5.cloned.1.call-done = f32[3072,1536]{1,0:T(8,128)} async-done(((f32[384,1536]{1,0:T(8,128)}), f32[3072,1536]{1,0:T(8,128)}) %all-gather.5.cloned.1.call-update) | async-done | bytes 18874384 | tf_op jit(solution)/shard_map/all_gather | solution.py:87
  462.1 4.3 fusion.7
  466.4 50.9 %reduce-scatter.7.cloned.1.call-done = f32[192,768]{1,0:T(8,128)} async-done(((f32[1536,768]{1,0:T(8,128)}), f32[192,768]{1,0:T(8,128)}) %reduce-scatter.7.cloned.1.call-update) | async-done | bytes 589840 | tf_op jit(solution)/shard_map/reduce_scatter | solution.py:95
  517.4 4.3 fusion.9
  521.7 51.2 %reduce-scatter.5.cloned.1.call-done = f32[192,768]{1,0:T(8,128)} async-done(((f32[1536,768]{1,0:T(8,128)}), f32[192,768]{1,0:T(8,128)}) %reduce-scatter.5.cloned.1.call-update) | async-done | bytes 589840 | tf_op jit(solution)/shard_map/reduce_scatter | solution.py:95
  572.9 4.3 fusion.31
  577.3 0.0 copy-start.8
  577.3 51.2 %reduce-scatter.11.cloned.1.call-done = f32[192,768]{1,0:T(8,128)} async-done(((f32[1536,768]{1,0:T(8,128)}), f32[192,768]{1,0:T(8,128)}) %reduce-scatter.11.cloned.1.call-update) | async-done | bytes 589840 | tf_op jit(solution)/shard_map/reduce_scatter | solution.py:95
  628.4 5.7 fusion.28
  634.1 0.0 all-reduce.2.cloned.1.call-update
  634.2 0.8 dynamic_slice.36
  634.9 52.2 %all-reduce.2.cloned.1.call-done = f32[192,1536]{1,0:T(8,128)} async-done(((f32[192,1536]{1,0:T(8,128)}), f32[192,1536]{1,0:T(8,128)}) %all-reduce.2.cloned.1.call-update) | async-done | bytes 1179664 | tf_op jit(solution)/shard_map/psum | solution.py:103
  687.1 0.0 copy-done.8
  687.1 7.8 %fusion.34 = f32[192,1536]{1,0:T(8,128)S(1)} fusion(f32[1536,1536]{1,0:T(8,128)} %all-gather.3.cloned.1.call-done, f32[192,1536]{1,0:T(8,128)} %all-reduce.2.cloned.1.call-done, f32[1536]{0:T(1024)S(1)} %copy-done.8, f32[192]{0:T(256)S(1)} %dynamic_slice.36, s32[1536]{0:T(1024)S(1)} %convert_reduce_fusion, s32[192]{0:T(256)S(1)} %copy-done.7, ...), kind=kOutput, calls=%fused_computation.26 | convolution fusion | flops 2720268288 | bytes 11811840 | tf_op jit(solution)/shard_map/dot_general | solution.py:17
  695.0 1.6 copy.14
  696.6 4.9 all-to-all-start
  701.5 0.1 dynamic_slice.38
  701.6 0.1 dynamic-slice_not_fusion
  701.7 3.1 pad_maximum_fusion
  704.8 1.3 negate_select_fusion
  706.1 33.2 %all-to-all-done = f32[192,8,192]{0,2,1:T(8,128)S(1)} async-done(((f32[192,8,192]{0,2,1:T(8,128)}), f32[192,8,192]{0,2,1:T(8,128)S(1)}, u32[]{:S(2)}, u32[]{:S(2)}) %all-to-all-start) | async-done | bytes 1179680 | tf_op jit(solution)/shard_map/all_to_all | solution.py:109
  739.3 0.9 copy.13
  740.2 0.5 all_to_all.17
  740.8 3.8 fusion.46
  (25 shorter events, 0.1 us)
Async XLA Ops:
  7.2 164.0 %all-gather.3.cloned.1.call-start = ((), (), s32[]{:S(2)}) async-start(), calls=%async_computation.5 | async-start | bytes 10616832 | tf_op jit(solution)/shard_map/all_gather | solution.py:76
  9.0 278.0 %copy-start.6 = (s32[192]{0:T(256)}, s32[192]{0:T(256)S(1)}, u32[]{:S(2)}) copy-start(s32[192]{0:T(256)S(1)} %dynamic_slice.31) | copy-start | bytes 2308
  9.6 2.7 copy-start.9
  9.6 161.5 %copy-start.13 = (f32[1536]{0:T(1024)}, f32[1536]{0:T(1024)S(1)}, u32[]{:S(2)}) copy-start(f32[1536]{0:T(1024)S(1)} %get-tuple-element.8) | copy-start | bytes 18436
  12.2 280.9 %reduce-scatter.9.cloned.1.call-start = ((), (), s32[]{:S(2)}) async-start(), calls=%async_computation.8 | async-start | bytes 5308416 | tf_op jit(solution)/shard_map/reduce_scatter | solution.py:95
  19.1 3.8 copy-start
  23.1 0.8 collective-permute-start
  23.9 177.0 %copy-start.4 = (f32[384,1536]{1,0:T(8,128)}, f32[384,1536]{1,0:T(8,128)S(1)}, u32[]{:S(2)}) copy-start(f32[384,1536]{1,0:T(8,128)S(1)} %collective-permute-done) | copy-start | bytes 7077892
  200.9 3.7 copy-start.14
  231.3 230.8 %all-gather.5.cloned.1.call-start = ((), (), s32[]{:S(2)}) async-start(), calls=%async_computation.10 | async-start | bytes 21233664 | tf_op jit(solution)/shard_map/all_gather | solution.py:87
  232.1 285.3 %reduce-scatter.7.cloned.1.call-start = ((), (), s32[]{:S(2)}) async-start(), calls=%async_computation.7 | async-start | bytes 5308416 | tf_op jit(solution)/shard_map/reduce_scatter | solution.py:95
  250.0 323.0 %reduce-scatter.5.cloned.1.call-start = ((), (), s32[]{:S(2)}) async-start(), calls=%async_computation.6 | async-start | bytes 5308416 | tf_op jit(solution)/shard_map/reduce_scatter | solution.py:95
  267.7 360.8 %reduce-scatter.11.cloned.1.call-start = ((), (), s32[]{:S(2)}) async-start(), calls=%async_computation.9 | async-start | bytes 5308416 | tf_op jit(solution)/shard_map/reduce_scatter | solution.py:95
  285.4 1.6 copy-start.5
  285.4 401.7 %all-reduce.2.cloned.1.call-start = ((), (), s32[]{:S(2)}) async-start(), calls=%async_computation.11 | async-start | bytes 2359296 | tf_op jit(solution)/shard_map/psum | solution.py:103
  285.8 180.7 %copy-start.11 = (s32[384]{0:T(512)}, s32[384]{0:T(512)S(1)}, u32[]{:S(2)}) copy-start(s32[384]{0:T(512)S(1)} %dynamic_slice.32) | copy-start | bytes 4612
  577.3 109.9 %copy-start.7 = (s32[192]{0:T(256)S(1)}, s32[192]{0:T(256)}, u32[]{:S(2)}) copy-start(s32[192]{0:T(256)} %copy-done.6) | copy-start | bytes 2308
  577.3 109.9 %copy-start.8 = (f32[1536]{0:T(1024)S(1)}, f32[1536]{0:T(1024)}, u32[]{:S(2)}) copy-start(f32[1536]{0:T(1024)} %get-tuple-element.6) | copy-start | bytes 18436
  577.3 109.9 %copy-start.10 = (pred[1536]{0:T(1024)(128)(4,1)S(1)}, pred[1536]{0:T(1024)(128)(4,1)}, u32[]{:S(2)}) copy-start(pred[1536]{0:T(1024)(128)(4,1)} %copy-done.9) | copy-start | bytes 4612
  695.0 1.7 copy-start.2
  695.0 6.7 copy-start.3
  695.0 9.8 %copy-start.1 = (f32[192,1536]{1,0:T(8,128)S(1)}, f32[192,1536]{1,0:T(8,128)}, u32[]{:S(2)}) copy-start(f32[192,1536]{1,0:T(8,128)} %all-reduce.2.cloned.1.call-done) | copy-start | bytes 3538948
  696.6 42.6 %all-to-all-start = ((f32[192,8,192]{0,2,1:T(8,128)}), f32[192,8,192]{0,2,1:T(8,128)S(1)}, u32[]{:S(2)}, u32[]{:S(2)}) async-start(f32[192,8,192]{0,2,1:T(8,128)} %bitcast.2), calls=%async_computation.4 | async-start | bytes 3145728 | tf_op jit(solution)/shard_map/all_to_all | solution.py:109
  704.8 36.0 %copy-start.12 = (s32[384]{0:T(512)S(1)}, s32[384]{0:T(512)}, u32[]{:S(2)}) copy-start(s32[384]{0:T(512)} %copy-done.11) | copy-start | bytes 4612
Sparse Core Ops, SparseCore 0:
  12.3 158.7 all-gather.2
  231.4 61.6 reduce-scatter.8
  295.3 166.7 all-gather.4
  464.3 53.0 reduce-scatter.6
  519.5 53.3 reduce-scatter.4
  575.1 53.3 reduce-scatter.10
  634.3 52.8 all-reduce.1
